TPU v7x, 32 devices: a whole 2x2x4 slice. The times are simulated.
32 devices in a mesh: groups: 2 (over x), replica: 2 (over core), tensor: 8 (over z, y).
Axes of the slice: x: 2, y: 2, z: 4, core: 2. Of those that a mesh axis runs over, the one named last changes fastest.
Arguments:
- hidden: bfloat16 [128, 8192], P(('groups', 'replica'), 'tensor'), parts along dimension 0, may hold values from -6 to 6
- w_query: bfloat16 [8192, 8192], P(None, 'tensor'), may hold values from -0.0625 to 0.0625
- output_weight: bfloat16 [8192, 8192], P('tensor'), may hold values from -0.09375 to 0.09375
- keys: bfloat16 [128, 8, 32, 128], P(('groups', 'replica')), parts along dimension 0
- values: bfloat16 [128, 8, 32, 128], P(('groups', 'replica')), parts along dimension 0, may hold values from -6 to 6
- query_down_maps: bfloat16 [16, 64, 8192], P(('groups', 'replica'), None, 'tensor'), parts along dimension 0, may hold values from -0.0625 to 0.0625
- query_up_maps: bfloat16 [16, 64, 8192], P(('groups', 'replica'), None, 'tensor'), parts along dimension 0, may hold values from -0.75 to 0.75
- output_down_maps: bfloat16 [16, 64, 8192], P(('groups', 'replica'), None, 'tensor'), parts along dimension 0, may hold values from -0.0625 to 0.0625
- output_up_maps: bfloat16 [16, 64, 8192], P(('groups', 'replica'), None, 'tensor'), parts along dimension 0, may hold values from -0.75 to 0.75
- adapter_ids: int32 [128], P('groups'), parts along dimension 0, may hold values from 0 to 7
- owner_map: int32 [16], P('groups'), parts along dimension 0, may hold values from 0 to 7, each once
- kv_lengths: int32 [128], P(('groups', 'replica')), parts along dimension 0, may hold values from 1 to 32, as said below
Outputs:
- attn_out: bfloat16 [128, 8192], P(('groups', 'replica'), 'tensor'), parts along dimension 0
There are 2 independent parts, one for each index of `groups`. A program takes and returns all parts, laid end to end along the dimension named above; an argument that names none is the same for every part. Nothing has to cross between parts.
Inputs may be any that keep to these rules, and one draw needn't show every extreme that they name: `owner_map`: every request's adapter has a slot; slot s is stored at replica index s // 4. Request r attends to its first kv_lengths[r] cached positions; some request holds all 32.
All inputs are finite; a program needn't handle non-finite values.
Results may differ from a plain program's by a relative error of at most 0.0092.
Values may be sent and summed in bfloat16 or wider, within the bound.
No kernel may reach another device: no remote copies, remote signals or barrier semaphores. Data moves between devices by JAX's collectives and lax.ppermute only.
A program may use at most 128 MiB of HBM per device.

v0:
```python
import math
import jax
import jax.numpy as jnp
from jax import lax
from jax.sharding import PartitionSpec as P

HEADS = 64
KVS = 8


def adapt(input_rows, slots, down_product, up_product):
    stored = down_product.shape[0]
    table = lax.broadcasted_iota(jnp.int32, (1, stored), 1)
    pick = (slots[:, None] == table).astype(jnp.bfloat16)
    part = jnp.einsum("ah,fth->aft", input_rows, down_product, preferred_element_type=jnp.float32)
    partial_value = jnp.sum(pick.astype(jnp.float32)[:, :, None] * part, axis=1)
    total = lax.psum(partial_value, "tensor")
    low = total.astype(jnp.bfloat16)
    spread_rows = pick[:, :, None] * low[:, None, :]
    return jnp.einsum("xpl,ply->xy", spread_rows, up_product, preferred_element_type=jnp.float32)


def per_device(
    hidden,
    w_query,
    output_weight,
    keys,
    values,
    query_down_maps,
    query_up_maps,
    output_down_maps,
    output_up_maps,
    adapter_ids,
    owner_map,
    kv_lengths,
):
    rows = hidden.shape[0]
    head_size = keys.shape[3]
    replica_at = lax.axis_index("replica")
    tensor_at = lax.axis_index("tensor")
    id_table = lax.broadcasted_iota(jnp.int32, (1, owner_map.shape[0]), 1)
    slots_all = jnp.sum(jnp.where(adapter_ids[:, None] == id_table, owner_map[None, :], 0), axis=1)
    own_slots = lax.dynamic_slice_in_dim(slots_all, replica_at * rows, rows)
    query_down_maps, query_up_maps, output_down_maps, output_up_maps = (
        lax.all_gather(query_down_maps, "replica", axis=0, tiled=True),
        lax.all_gather(query_up_maps, "replica", axis=0, tiled=True),
        lax.all_gather(output_down_maps, "replica", axis=0, tiled=True),
        lax.all_gather(output_up_maps, "replica", axis=0, tiled=True),
    )

    def apply_adapter(input_rows, down_product, up_product):
        return adapt(input_rows, own_slots, down_product, up_product)

    plain_projection = jnp.dot(
        lax.all_gather(hidden, "tensor", axis=1, tiled=True),
        w_query,
        preferred_element_type=jnp.float32,
    )
    query_rows = (
        plain_projection + 0.5 * apply_adapter(hidden, query_down_maps, query_up_maps)
    ).astype(jnp.bfloat16)
    local_heads = query_rows.shape[1] // head_size
    group = HEADS // KVS
    kv_count = max(1, local_heads // group)
    first_kv = tensor_at * local_heads // group
    key_block = lax.dynamic_slice_in_dim(keys, first_kv, kv_count, 1)
    value_block = lax.dynamic_slice_in_dim(values, first_kv, kv_count, 1)
    heads_q = query_rows.reshape(rows, kv_count, local_heads // kv_count, head_size)
    scores = jnp.einsum(
        "rkhd,rkld->rkhl", heads_q, key_block, preferred_element_type=jnp.float32
    ) / math.sqrt(head_size)
    live = (
        lax.broadcasted_iota(jnp.int32, (rows, 1, 1, keys.shape[2]), 3)
        < kv_lengths[:, None, None, None]
    )
    scores = jnp.where(live, scores, -1e30)
    top = jnp.max(scores, axis=-1, keepdims=True)
    weights = jnp.exp(scores - top)
    probs = (weights / jnp.sum(weights, axis=-1, keepdims=True)).astype(jnp.bfloat16)
    combined_output = jnp.einsum(
        "rkhl,rkld->rkhd", probs, value_block, preferred_element_type=jnp.float32
    )
    combined_output = combined_output.astype(jnp.bfloat16).reshape(rows, -1)
    partial_value = jnp.dot(combined_output, output_weight, preferred_element_type=jnp.float32)
    out_base = lax.psum_scatter(partial_value, "tensor", scatter_dimension=1, tiled=True)
    final_output = out_base + 0.5 * apply_adapter(combined_output, output_down_maps, output_up_maps)
    return final_output.astype(jnp.bfloat16)


def solution(mesh):
    return jax.shard_map(
        per_device,
        mesh=mesh,
        in_specs=(
            P(("groups", "replica"), "tensor"),
            P(None, "tensor"),
            P("tensor", None),
            P(("groups", "replica"), None, None, None),
            P(("groups", "replica"), None, None, None),
            P(("groups", "replica"), None, "tensor"),
            P(("groups", "replica"), None, "tensor"),
            P(("groups", "replica"), None, "tensor"),
            P(("groups", "replica"), None, "tensor"),
            P("groups"),
            P("groups"),
            P(("groups", "replica")),
        ),
        out_specs=P(("groups", "replica"), "tensor"),
        check_vma=False,
    )
```

profile of v0, /device:TPU:0, one launch (start us, length us, event | category | flops | bytes accessed | tf_op | source)
XLA Modules:
  0.0 174.8 jit_solution(11398326931381532155)
XLA Ops:
  6.5 0.0 copy-start
  6.5 0.0 copy-start.4
  6.5 0.0 copy-start.3
  6.5 0.0 copy-start.1
  6.5 0.0 copy-start.2
  6.5 0.0 all-gather.5.cloned.1.call-start
  6.6 0.7 all-gather.5.cloned.1.call-update
  7.3 0.0 all-gather.7.cloned.1.call-start
  7.3 0.7 all-gather.7.cloned.1.call-update
  8.0 0.0 all-gather.9.cloned.1.call-start
  8.1 0.7 all-gather.9.cloned.1.call-update
  8.8 0.0 all-gather.11.cloned.1.call-start
  8.8 0.5 all-gather.11.cloned.1.call-update
  9.3 0.0 reduce-scatter.2.cloned.1.call-start
  9.4 0.0 copy-done.4
  9.4 0.0 copy-done.3
  9.4 0.1 select_reduce_fusion
  9.5 0.1 dynamic_slice.9
  9.6 0.0 copy-done.1
  9.6 33.0 %all_gather.15 = bf16[32,8192]{1,0:T(8,128)(2,1)S(1)} all-gather(bf16[32,1024]{1,0:T(8,128)(2,1)S(1)} %copy-done.1), channel_id=1, replica_groups=mesh['groups'=2,'replica'=2,'tensor'=8] {'tensor'}, dimensions={1}, use_global_device_ids=true | all-gather | bytes 589824 | tf_op jit(solution)/shard_map/all_gather | solution.py:55
  42.6 0.0 copy-done.2
  42.6 0.1 iota_compare_fusion
  42.7 8.7 %fusion.55 = f32[32,1024]{1,0:T(8,128)S(1)} fusion(bf16[32,8192]{1,0:T(8,128)(2,1)S(1)} %all_gather.15, bf16[8192,1024]{1,0:T(8,128)(2,1)} %param.13), kind=kOutput, calls=%fused_computation.51 | convolution fusion | flops 536870912 | bytes 17432576 | tf_op jit(solution)/shard_map/dot_general | solution.py:54
  51.5 0.0 all-gather.5.cloned.1.call-done
  51.5 1.8 %fusion.10 = f32[32,64]{1,0:T(8,128)S(1)} fusion(bf16[8,64,1024]{2,1,0:T(8,128)(2,1)} %all-gather.5.cloned.1.call-done, bf16[32,1024]{1,0:T(8,128)(2,1)S(1)} %copy-done.1, f32[32,8]{0,1:T(8,128)S(1)} %get-tuple-element.6), kind=kOutput, calls=%fused_computation.16 | convolution fusion | flops 33585152 | bytes 1123328 | tf_op jit(solution)/shard_map/ah,fth->aft/dot_general | solution.py:15
  53.3 37.4 %psum.14 = bf16[32,64]{1,0:T(8,128)(2,1)S(1)} all-reduce(f32[32,64]{1,0:T(8,128)S(1)} %fusion.10), channel_id=1, replica_groups=mesh['groups'=2,'replica'=2,'tensor'=8] {'tensor'}, use_global_device_ids=true, to_apply=%region_2.3 | all-reduce | flops 2048 | bytes 12288 | tf_op jit(solution)/shard_map/psum | solution.py:17
  90.7 0.0 all-gather.7.cloned.1.call-done
  90.7 1.6 fusion.12
  92.3 0.0 copy-done
  92.3 0.4 fusion.52
  92.8 1.5 convolution_convert_fusion
  94.3 9.8 %fusion.17 = f32[32,8192]{1,0:T(8,128)} fusion(bf16[1024,8192]{1,0:T(8,128)(2,1)} %param.14, bf16[4,8,8,128]{3,2,1,0:T(8,128)(2,1)S(1)} %bitcast.54), kind=kOutput, calls=%fused_computation.24 | convolution fusion | flops 536870912 | bytes 17891328 | tf_op jit(solution)/shard_map/dot_general | solution.py:84
  104.0 0.0 reduce-scatter.2.cloned.1.call-update
  104.1 0.0 all-gather.9.cloned.1.call-done
  104.1 1.8 %fusion.11 = f32[32,64]{1,0:T(8,128)S(1)} fusion(bf16[32,1024,1]{1,0,2:T(8,128)(2,1)S(1)} %reshape.106, bf16[8,64,1024]{2,1,0:T(8,128)(2,1)} %all-gather.9.cloned.1.call-done, f32[32,8]{0,1:T(8,128)S(1)} %get-tuple-element.6), kind=kOutput, calls=%fused_computation.17 | convolution fusion | flops 33585152 | bytes 1123328 | tf_op jit(solution)/shard_map/ah,fth->aft/dot_general | solution.py:15
  106.0 33.3 %psum.15 = bf16[32,64]{1,0:T(8,128)(2,1)S(1)} all-reduce(f32[32,64]{1,0:T(8,128)S(1)} %fusion.11), channel_id=1, replica_groups=mesh['groups'=2,'replica'=2,'tensor'=8] {'tensor'}, use_global_device_ids=true, to_apply=%region_7.8 | all-reduce | flops 2048 | bytes 12288 | tf_op jit(solution)/shard_map/psum | solution.py:17
  139.2 0.0 all-gather.11.cloned.1.call-done
  139.2 26.8 %reduce-scatter.2.cloned.1.call-done = f32[32,1024]{1,0:T(8,128)} async-done(((f32[32,8192]{1,0:T(8,128)}), f32[32,1024]{1,0:T(8,128)}) %reduce-scatter.2.cloned.1.call-update) | async-done | bytes 131088 | tf_op jit(solution)/shard_map/reduce_scatter | solution.py:85
  166.1 2.2 %fusion.8 = bf16[32,1024]{1,0:T(8,128)(2,1)} fusion(f32[32,1024]{1,0:T(8,128)} %reduce-scatter.2.cloned.1.call-done, bf16[8,64,1024]{2,1,0:T(8,128)(2,1)} %all-gather.11.cloned.1.call-done, bf16[32,64]{1,0:T(8,128)(2,1)S(1)} %psum.15, bf16[32,8]{0,1:T(8,128)(2,1)S(1)} %get-tuple-element.5), kind=kOutput, calls=%fused_computation.13 | convolution fusion | flops 33669120 | bytes 1249792 | tf_op jit(solution)/shard_map/xpl,ply->xy/dot_general | solution.py:20
  (3 shorter events, 0.1 us)
Async XLA Ops:
  6.5 85.8 %copy-start = (bf16[32,8,32,128]{3,2,1,0:T(8,128)(2,1)S(1)}, bf16[32,8,32,128]{3,2,1,0:T(8,128)(2,1)}, u32[]{:S(2)}) copy-start(bf16[32,8,32,128]{3,2,1,0:T(8,128)(2,1)} %param.15) | copy-start | bytes 6291460
  6.5 2.9 %copy-start.4 = (s32[64]{0:T(128)S(1)}, s32[64]{0:T(128)}, u32[]{:S(2)}) copy-start(s32[64]{0:T(128)} %param.21) | copy-start | bytes 772
  6.5 2.9 %copy-start.3 = (s32[8]{0:T(128)S(1)}, s32[8]{0:T(128)}, u32[]{:S(2)}) copy-start(s32[8]{0:T(128)} %param.22) | copy-start | bytes 100
  6.5 3.1 %copy-start.1 = (bf16[32,1024]{1,0:T(8,128)(2,1)S(1)}, bf16[32,1024]{1,0:T(8,128)(2,1)}, u32[]{:S(2)}) copy-start(bf16[32,1024]{1,0:T(8,128)(2,1)} %param.12) | copy-start | bytes 196612
  6.5 36.1 %copy-start.2 = (s32[32]{0:T(128)S(1)}, s32[32]{0:T(128)}, u32[]{:S(2)}) copy-start(s32[32]{0:T(128)} %param.23) | copy-start | bytes 388
  6.5 44.9 %all-gather.5.cloned.1.call-start = ((), (), s32[]{:S(2)}) async-start(), calls=%async_computation.1 | async-start | bytes 1572864 | tf_op jit(solution)/shard_map/all_gather | solution.py:45
  7.3 83.4 %all-gather.7.cloned.1.call-start = ((), (), s32[]{:S(2)}) async-start(), calls=%async_computation.2 | async-start | bytes 1572864 | tf_op jit(solution)/shard_map/all_gather | solution.py:46
  8.0 96.1 %all-gather.9.cloned.1.call-start = ((), (), s32[]{:S(2)}) async-start(), calls=%async_computation.4 | async-start | bytes 1572864 | tf_op jit(solution)/shard_map/all_gather | solution.py:47
  8.8 130.4 %all-gather.11.cloned.1.call-start = ((), (), s32[]{:S(2)}) async-start(), calls=%async_computation.5 | async-start | bytes 1572864 | tf_op jit(solution)/shard_map/all_gather | solution.py:48
  9.3 156.7 %reduce-scatter.2.cloned.1.call-start = ((), (), s32[]{:S(2)}) async-start(), calls=%async_computation.3 | async-start | bytes 1179648 | tf_op jit(solution)/shard_map/reduce_scatter | solution.py:85
Sparse Core Ops, SparseCore 0:
  8.9 11.7 all-gather.4
  22.2 10.1 all-gather.6
  34.0 10.1 all-gather.8
  45.6 10.2 all-gather.10
  104.2 61.8 reduce-scatter.1
where the time goes:
time: 175 us
  blocking collectives  104 us (59%)
  waiting for transfers between devices  29.5 us (17%)
  matrix products  28 us (16%)
  between operations  13.2 us (8%)
    psum x2, blocking collectives, adapt(): total = lax.psum(partial_value, 'tensor')  70.6 us
    all_gather x1, blocking collectives, per_device(): lax.all_gather(hidden, 'tensor', axis=1, tiled=True)  33 us
    reduce_scatter x1, waiting for transfers between devices, per_device(): lax.psum_scatter(partial_value, 'tensor', scatter_dimension=1, tiled=True)  26.8 us
    dot_general x1, matrix products, per_device(): jnp.dot(combined_output, output_weight, preferred_element_type=jnp.float32)  9.75 us
    dot_general x1, matrix products, per_device(): jnp.dot(lax.all_gather(hidden, 'tensor', axis=1, tiled=True), w_query, pr...  8.75 us
    dot_general x2, matrix products, adapt(): jnp.einsum('xpl,ply->xy', spread_rows, up_product, preferred_element_type...  3.86 us
    dot_general x2, matrix products, adapt(): jnp.einsum('ah,fth->aft', input_rows, down_product, preferred_element_typ...  3.67 us
  transfers between devices with their start and end apart: 5, of which 1 were waited for; matrix products, arithmetic and copies ran while one was open for 15% of the time, Pallas kernels for 0%

commit v1 on v0

--- a/solution.py
+++ b/solution.py
@@ -14,7 +14,11 @@
     pick = (slots[:, None] == table).astype(jnp.bfloat16)
     part = jnp.einsum("ah,fth->aft", input_rows, down_product, preferred_element_type=jnp.float32)
     partial_value = jnp.sum(pick.astype(jnp.float32)[:, :, None] * part, axis=1)
-    total = lax.psum(partial_value, "tensor")
+    size = lax.axis_size("tensor")
+    total, far = (partial_value, 1)
+    while far < size:
+        total = total + lax.ppermute(total, "tensor", [(i, i ^ far) for i in range(size)])
+        far = 2 * far
     low = total.astype(jnp.bfloat16)
     spread_rows = pick[:, :, None] * low[:, None, :]
     return jnp.einsum("xpl,ply->xy", spread_rows, up_product, preferred_element_type=jnp.float32)

time: 175 us -> 157 us (0.90)
  blocking collectives: 104 us -> 31.5 us
  waiting for transfers between devices: 29.5 us -> 74.8 us
  starting transfers between devices: 0.19 us -> 8.88 us
    psum x2 -> x0, blocking collectives: 70.6 us -> none  [adapt(): total = lax.psum(partial_value, 'tensor')]
    reduce_scatter x1, waiting for transfers between devices: 26.8 us -> 51 us  [per_device(): lax.psum_scatter(partial_value, 'tensor', scatter_dimension=1, tiled=True)]
    all_gather x1, waiting for transfers between devices: 0.01 us -> 11.1 us  [per_device(): lax.all_gather(query_down_maps, 'replica', axis=0, tiled=True)]
    ppermute x0 -> x6, waiting for transfers between devices: none -> 10 us  [adapt(): lax.ppermute(total, 'tensor', [(i, i ^ far) for i in range(size)])]
    ppermute x0 -> x6, starting transfers between devices: none -> 8.7 us  [adapt(): lax.ppermute(total, 'tensor', [(i, i ^ far) for i in range(size)])]
  transfers between devices with their start and end apart: 5 -> 11, of which waited for: 1 -> 6; matrix products, arithmetic and copies ran while one was open for 15% -> 17% of each run, Pallas kernels for 0% -> 0%
where the time goes in v1:
time: 157 us
  waiting for transfers between devices  74.8 us (48%)
  blocking collectives  31.5 us (20%)
  matrix products  28 us (18%)
  between operations  13.3 us (8%)
  starting transfers between devices  8.88 us (6%)
    reduce_scatter x1, waiting for transfers between devices, per_device(): lax.psum_scatter(partial_value, 'tensor', scatter_dimension=1, tiled=True)  51 us
    all_gather x1, blocking collectives, per_device(): lax.all_gather(hidden, 'tensor', axis=1, tiled=True)  31.5 us
    all_gather x1, waiting for transfers between devices, per_device(): lax.all_gather(query_down_maps, 'replica', axis=0, tiled=True)  11.1 us
    ppermute x6, waiting for transfers between devices, adapt(): lax.ppermute(total, 'tensor', [(i, i ^ far) for i in range(size)])  10 us
    dot_general x1, matrix products, per_device(): jnp.dot(combined_output, output_weight, preferred_element_type=jnp.float32)  9.77 us
    dot_general x1, matrix products, per_device(): jnp.dot(lax.all_gather(hidden, 'tensor', axis=1, tiled=True), w_query, pr...  8.75 us
    ppermute x6, starting transfers between devices, adapt(): lax.ppermute(total, 'tensor', [(i, i ^ far) for i in range(size)])  8.7 us
    dot_general x2, matrix products, adapt(): jnp.einsum('xpl,ply->xy', spread_rows, up_product, preferred_element_type...  3.87 us
  transfers between devices with their start and end apart: 11, of which 6 were waited for; matrix products, arithmetic and copies ran while one was open for 17% of the time, Pallas kernels for 0%

profile of v1, /device:TPU:0, one launch (start us, length us, event | category | flops | bytes accessed | tf_op | source)
XLA Modules:
  0.0 156.8 jit_solution(5544614882770334121)
XLA Ops:
  6.5 0.0 copy-start
  6.5 0.0 copy-start.4
  6.5 0.0 copy-start.3
  6.5 0.0 copy-start.1
  6.5 0.0 all-gather.5.cloned.1.call-start
  6.6 0.7 all-gather.5.cloned.1.call-update
  7.3 0.0 all-gather.7.cloned.1.call-start
  7.3 0.7 all-gather.7.cloned.1.call-update
  8.0 0.0 all-gather.9.cloned.1.call-start
  8.1 0.7 all-gather.9.cloned.1.call-update
  8.8 0.0 all-gather.11.cloned.1.call-start
  8.8 0.5 all-gather.11.cloned.1.call-update
  9.3 0.0 reduce-scatter.2.cloned.1.call-start
  9.4 0.0 copy-done.4
  9.4 0.0 copy-done.3
  9.4 0.1 select_reduce_fusion
  9.5 0.1 dynamic_slice.9
  9.6 11.1 %all-gather.5.cloned.1.call-done = bf16[8,64,1024]{2,1,0:T(8,128)(2,1)} async-done(((bf16[4,64,1024]{2,1,0:T(8,128)(2,1)}), bf16[8,64,1024]{2,1,0:T(8,128)(2,1)}) %all-gather.5.cloned.1.call-update) | async-done | bytes 1048592 | tf_op jit(solution)/shard_map/all_gather | solution.py:49
  20.7 0.0 copy-done.1
  20.7 1.8 %fusion.10 = f32[32,64]{1,0:T(8,128)S(1)} fusion(bf16[8,64,1024]{2,1,0:T(8,128)(2,1)} %all-gather.5.cloned.1.call-done, bf16[32,1024]{1,0:T(8,128)(2,1)S(1)} %copy-done.1, f32[32,8]{0,1:T(8,128)S(1)} %get-tuple-element.6), kind=kOutput, calls=%fused_computation.16 | convolution fusion | flops 33585152 | bytes 1123328 | tf_op jit(solution)/shard_map/ah,fth->aft/dot_general | solution.py:15
  22.5 1.8 %collective-permute-start = (f32[32,64]{1,0:T(8,128)S(1)}, f32[32,64]{1,0:T(8,128)S(1)}, u32[]{:S(2)}, u32[]{:S(2)}) collective-permute-start(f32[32,64]{1,0:T(8,128)S(1)} %fusion.10), channel_id=1, source_target_pairs={{0,1},{1,0},{2,3},{3,2},{4,5},{5,4},{6,7},{7,6},{8,9},{9,8},{10,11... | collective-permute-start | bytes 24584 | tf_op jit(solution)/shard_map/ppermute | solution.py:20
  24.3 31.5 %all_gather.15 = bf16[32,8192]{1,0:T(8,128)(2,1)S(1)} all-gather(bf16[32,1024]{1,0:T(8,128)(2,1)S(1)} %copy-done.1), channel_id=1, replica_groups=mesh['groups'=2,'replica'=2,'tensor'=8] {'tensor'}, dimensions={1}, use_global_device_ids=true | all-gather | bytes 589824 | tf_op jit(solution)/shard_map/all_gather | solution.py:59
  55.8 0.0 collective-permute-done
  55.8 0.0 copy-start.2
  55.9 0.1 collective-permute-start.1
  55.9 8.7 %fusion.55 = f32[32,1024]{1,0:T(8,128)S(1)} fusion(bf16[32,8192]{1,0:T(8,128)(2,1)S(1)} %all_gather.15, bf16[8192,1024]{1,0:T(8,128)(2,1)} %param.13), kind=kOutput, calls=%fused_computation.53 | convolution fusion | flops 536870912 | bytes 17432576 | tf_op jit(solution)/shard_map/dot_general | solution.py:58
  64.7 0.0 collective-permute-done.1
  64.7 1.2 collective-permute-start.2
  65.9 0.0 copy-done.2
  65.9 0.1 iota_compare_fusion
  66.0 3.4 %collective-permute-done.2 = f32[32,64]{1,0:T(8,128)S(1)} collective-permute-done((f32[32,64]{1,0:T(8,128)S(1)}, f32[32,64]{1,0:T(8,128)S(1)}, u32[]{:S(2)}, u32[]{:S(2)}) %collective-permute-start.2) | collective-permute-done | bytes 8224 | tf_op jit(solution)/shard_map/ppermute | solution.py:20
  69.4 0.0 all-gather.7.cloned.1.call-done
  69.4 1.6 %fusion.12 = bf16[4,8,8,128]{3,1,2,0:T(8,128)(2,1)S(1)} fusion(f32[32,1024]{1,0:T(8,128)S(1)} %fusion.55, bf16[8,64,1024]{2,1,0:T(8,128)(2,1)} %all-gather.7.cloned.1.call-done, bf16[32,64]{1,0:T(8,128)(2,1)S(1)} %add_convert_fusion.1, bf16[32,8]{0,1:T(8,128)(2,1)S(1)} %get-tuple-element.5), kind=kOutput, calls=%fused_computation.18 | convolution fusion | flops 33669120 | bytes 1249792 | tf_op jit(solution)/shard_map/xpl,ply->xy/dot_general | solution.py:24
  71.1 0.0 copy-done
  71.1 0.4 fusion.52
  71.5 1.5 convolution_convert_fusion
  73.0 9.8 %fusion.17 = f32[32,8192]{1,0:T(8,128)} fusion(bf16[1024,8192]{1,0:T(8,128)(2,1)} %param.14, bf16[4,8,8,128]{3,2,1,0:T(8,128)(2,1)S(1)} %bitcast.54), kind=kOutput, calls=%fused_computation.24 | convolution fusion | flops 536870912 | bytes 17891328 | tf_op jit(solution)/shard_map/dot_general | solution.py:88
  82.8 0.0 reduce-scatter.2.cloned.1.call-update
  82.8 0.0 all-gather.9.cloned.1.call-done
  82.9 1.8 %fusion.11 = f32[32,64]{1,0:T(8,128)S(1)} fusion(bf16[32,1024,1]{1,0,2:T(8,128)(2,1)S(1)} %reshape.106, bf16[8,64,1024]{2,1,0:T(8,128)(2,1)} %all-gather.9.cloned.1.call-done, f32[32,8]{0,1:T(8,128)S(1)} %get-tuple-element.6), kind=kOutput, calls=%fused_computation.17 | convolution fusion | flops 33585152 | bytes 1123328 | tf_op jit(solution)/shard_map/ah,fth->aft/dot_general | solution.py:15
  84.7 1.4 collective-permute-start.3
  86.1 2.4 %collective-permute-done.3 = f32[32,64]{1,0:T(8,128)S(1)} collective-permute-done((f32[32,64]{1,0:T(8,128)S(1)}, f32[32,64]{1,0:T(8,128)S(1)}, u32[]{:S(2)}, u32[]{:S(2)}) %collective-permute-start.3) | collective-permute-done | bytes 8224 | tf_op jit(solution)/shard_map/ppermute | solution.py:20
  88.5 2.0 %collective-permute-start.4 = (f32[32,64]{1,0:T(8,128)S(1)}, f32[32,64]{1,0:T(8,128)S(1)}, u32[]{:S(2)}, u32[]{:S(2)}) collective-permute-start(f32[32,64]{1,0:T(8,128)S(1)} %add.40), channel_id=1, source_target_pairs={{0,2},{1,3},{2,0},{3,1},{4,6},{5,7},{6,4},{7,5},{8,10},{9,11},{10,... | collective-permute-start | bytes 24584 | tf_op jit(solution)/shard_map/ppermute | solution.py:20
  90.5 1.7 %collective-permute-done.4 = f32[32,64]{1,0:T(8,128)S(1)} collective-permute-done((f32[32,64]{1,0:T(8,128)S(1)}, f32[32,64]{1,0:T(8,128)S(1)}, u32[]{:S(2)}, u32[]{:S(2)}) %collective-permute-start.4) | collective-permute-done | bytes 8224 | tf_op jit(solution)/shard_map/ppermute | solution.py:20
  92.2 2.2 %collective-permute-start.5 = (f32[32,64]{1,0:T(8,128)S(1)}, f32[32,64]{1,0:T(8,128)S(1)}, u32[]{:S(2)}, u32[]{:S(2)}) collective-permute-start(f32[32,64]{1,0:T(8,128)S(1)} %add.41), channel_id=1, source_target_pairs={{0,4},{1,5},{2,6},{3,7},{4,0},{5,1},{6,2},{7,3},{8,12},{9,13},{10,... | collective-permute-start | bytes 24584 | tf_op jit(solution)/shard_map/ppermute | solution.py:20
  94.5 2.4 %collective-permute-done.5 = f32[32,64]{1,0:T(8,128)S(1)} collective-permute-done((f32[32,64]{1,0:T(8,128)S(1)}, f32[32,64]{1,0:T(8,128)S(1)}, u32[]{:S(2)}, u32[]{:S(2)}) %collective-permute-start.5) | collective-permute-done | bytes 8224 | tf_op jit(solution)/shard_map/ppermute | solution.py:20
  96.9 0.0 all-gather.11.cloned.1.call-done
  96.9 51.0 %reduce-scatter.2.cloned.1.call-done = f32[32,1024]{1,0:T(8,128)} async-done(((f32[32,8192]{1,0:T(8,128)}), f32[32,1024]{1,0:T(8,128)}) %reduce-scatter.2.cloned.1.call-update) | async-done | bytes 131088 | tf_op jit(solution)/shard_map/reduce_scatter | solution.py:89
  148.0 2.2 %fusion.8 = bf16[32,1024]{1,0:T(8,128)(2,1)} fusion(f32[32,1024]{1,0:T(8,128)} %reduce-scatter.2.cloned.1.call-done, bf16[8,64,1024]{2,1,0:T(8,128)(2,1)} %all-gather.11.cloned.1.call-done, bf16[32,64]{1,0:T(8,128)(2,1)S(1)} %add_convert_fusion, bf16[32,8]{0,1:T(8,128)(2,1)S(1)} %get-tuple-element.5), kind=kOutput, calls=%fused_computation.13 | convolution fusion | flops 33669120 | bytes 1249792 | tf_op jit(solution)/shard_map/xpl,ply->xy/dot_general | solution.py:24
  (9 shorter events, 0.1 us)
Async XLA Ops:
  6.5 64.5 %copy-start = (bf16[32,8,32,128]{3,2,1,0:T(8,128)(2,1)S(1)}, bf16[32,8,32,128]{3,2,1,0:T(8,128)(2,1)}, u32[]{:S(2)}) copy-start(bf16[32,8,32,128]{3,2,1,0:T(8,128)(2,1)} %param.15) | copy-start | bytes 6291460
  6.5 2.9 %copy-start.4 = (s32[64]{0:T(128)S(1)}, s32[64]{0:T(128)}, u32[]{:S(2)}) copy-start(s32[64]{0:T(128)} %param.21) | copy-start | bytes 772
  6.5 2.9 %copy-start.3 = (s32[8]{0:T(128)S(1)}, s32[8]{0:T(128)}, u32[]{:S(2)}) copy-start(s32[8]{0:T(128)} %param.22) | copy-start | bytes 100
  6.5 14.1 %copy-start.1 = (bf16[32,1024]{1,0:T(8,128)(2,1)S(1)}, bf16[32,1024]{1,0:T(8,128)(2,1)}, u32[]{:S(2)}) copy-start(bf16[32,1024]{1,0:T(8,128)(2,1)} %param.12) | copy-start | bytes 196612
  6.5 14.1 %all-gather.5.cloned.1.call-start = ((), (), s32[]{:S(2)}) async-start(), calls=%async_computation.1 | async-start | bytes 1572864 | tf_op jit(solution)/shard_map/all_gather | solution.py:49
  7.3 62.1 %all-gather.7.cloned.1.call-start = ((), (), s32[]{:S(2)}) async-start(), calls=%async_computation.2 | async-start | bytes 1572864 | tf_op jit(solution)/shard_map/all_gather | solution.py:50
  8.0 74.8 %all-gather.9.cloned.1.call-start = ((), (), s32[]{:S(2)}) async-start(), calls=%async_computation.4 | async-start | bytes 1572864 | tf_op jit(solution)/shard_map/all_gather | solution.py:51
  8.8 88.2 %all-gather.11.cloned.1.call-start = ((), (), s32[]{:S(2)}) async-start(), calls=%async_computation.5 | async-start | bytes 1572864 | tf_op jit(solution)/shard_map/all_gather | solution.py:52
  9.3 138.6 %reduce-scatter.2.cloned.1.call-start = ((), (), s32[]{:S(2)}) async-start(), calls=%async_computation.3 | async-start | bytes 1179648 | tf_op jit(solution)/shard_map/reduce_scatter | solution.py:89
  22.5 33.3 %collective-permute-start = (f32[32,64]{1,0:T(8,128)S(1)}, f32[32,64]{1,0:T(8,128)S(1)}, u32[]{:S(2)}, u32[]{:S(2)}) collective-permute-start(f32[32,64]{1,0:T(8,128)S(1)} %fusion.10), channel_id=1, source_target_pairs={{0,1},{1,0},{2,3},{3,2},{4,5},{5,4},{6,7},{7,6},{8,9},{9,8},{10,11... | collective-permute-start | bytes 24584 | tf_op jit(solution)/shard_map/ppermute | solution.py:20
  55.8 10.1 %copy-start.2 = (s32[32]{0:T(128)S(1)}, s32[32]{0:T(128)}, u32[]{:S(2)}) copy-start(s32[32]{0:T(128)} %param.23) | copy-start | bytes 388
  55.9 8.8 %collective-permute-start.1 = (f32[32,64]{1,0:T(8,128)S(1)}, f32[32,64]{1,0:T(8,128)S(1)}, u32[]{:S(2)}, u32[]{:S(2)}) collective-permute-start(f32[32,64]{1,0:T(8,128)S(1)} %add.35), channel_id=1, source_target_pairs={{0,2},{1,3},{2,0},{3,1},{4,6},{5,7},{6,4},{7,5},{8,10},{9,11},{10,... | collective-permute-start | bytes 24584 | tf_op jit(solution)/shard_map/ppermute | solution.py:20
  64.7 4.7 %collective-permute-start.2 = (f32[32,64]{1,0:T(8,128)S(1)}, f32[32,64]{1,0:T(8,128)S(1)}, u32[]{:S(2)}, u32[]{:S(2)}) collective-permute-start(f32[32,64]{1,0:T(8,128)S(1)} %add.36), channel_id=1, source_target_pairs={{0,4},{1,5},{2,6},{3,7},{4,0},{5,1},{6,2},{7,3},{8,12},{9,13},{10,... | collective-permute-start | bytes 24584 | tf_op jit(solution)/shard_map/ppermute | solution.py:20
  84.7 3.8 %collective-permute-start.3 = (f32[32,64]{1,0:T(8,128)S(1)}, f32[32,64]{1,0:T(8,128)S(1)}, u32[]{:S(2)}, u32[]{:S(2)}) collective-permute-start(f32[32,64]{1,0:T(8,128)S(1)} %fusion.11), channel_id=1, source_target_pairs={{0,1},{1,0},{2,3},{3,2},{4,5},{5,4},{6,7},{7,6},{8,9},{9,8},{10,11... | collective-permute-start | bytes 24584 | tf_op jit(solution)/shard_map/ppermute | solution.py:20
  88.5 3.7 %collective-permute-start.4 = (f32[32,64]{1,0:T(8,128)S(1)}, f32[32,64]{1,0:T(8,128)S(1)}, u32[]{:S(2)}, u32[]{:S(2)}) collective-permute-start(f32[32,64]{1,0:T(8,128)S(1)} %add.40), channel_id=1, source_target_pairs={{0,2},{1,3},{2,0},{3,1},{4,6},{5,7},{6,4},{7,5},{8,10},{9,11},{10,... | collective-permute-start | bytes 24584 | tf_op jit(solution)/shard_map/ppermute | solution.py:20
  92.2 4.7 %collective-permute-start.5 = (f32[32,64]{1,0:T(8,128)S(1)}, f32[32,64]{1,0:T(8,128)S(1)}, u32[]{:S(2)}, u32[]{:S(2)}) collective-permute-start(f32[32,64]{1,0:T(8,128)S(1)} %add.41), channel_id=1, source_target_pairs={{0,4},{1,5},{2,6},{3,7},{4,0},{5,1},{6,2},{7,3},{8,12},{9,13},{10,... | collective-permute-start | bytes 24584 | tf_op jit(solution)/shard_map/ppermute | solution.py:20
Sparse Core Ops, SparseCore 0:
  8.9 11.7 all-gather.4
  22.2 10.1 all-gather.6
  34.0 10.1 all-gather.8
  45.6 10.1 all-gather.10
  82.9 65.0 reduce-scatter.1
